TPU v7x, 256 devices: a whole 4x4x8 slice. The times are simulated.
256 devices in a mesh: chain: 8 (over x, core), col: 32 (over y, z).
Axes of the slice: x: 4, y: 4, z: 8, core: 2. Of those that a mesh axis runs over, the one named last changes fastest.
Arguments:
- rhs: float32 [8, 32, 64, 128], P('chain', 'col'), may hold values from -6 to 6
- inverse: float32 [8, 32, 128, 128], P('chain', 'col'), as said below
- factor: float32 [8, 32, 8, 128, 128], P('chain', 'col'), may hold values from -0.1875 to 0.1875
- pattern: int32 [8, 32, 8], P('chain', 'col'), may hold values from 0 to 31, as said below
Outputs:
- forward: float32 [8, 32, 64, 128], P('chain', 'col')
- solution: float32 [8, 32, 64, 128], P('chain', 'col')
Inputs may be any that keep to these rules, and one draw needn't show every extreme that they name: `pattern`: the 8 block rows of one supernode are distinct. `inverse`: each block is lower triangular, its diagonal between 0.5 and 1.5.
All inputs are finite; a program needn't handle non-finite values.
Results may differ from a plain program's by a relative error of at most 0.00012.
Values sent between devices are 32-bit elements; how exact they have to be, the bound alone decides.
No kernel may reach another device: no remote copies, remote signals or barrier semaphores. Data moves between devices by JAX's collectives and lax.ppermute only.
A program may use at most 64 MiB of HBM per device.

v0:
```python
import jax
import jax.numpy as jnp
from jax import lax
from jax.sharding import PartitionSpec as P


def shifted(value, axis, steps):
    count = lax.axis_size(axis)
    first, last = (max(0, -steps), min(count, count - steps))
    return lax.ppermute(value, axis, [(source, source + steps) for source in range(first, last)])


def body(rhs, inverse, factor, pattern):
    levels = lax.axis_size("chain")
    supers = lax.axis_size("col")
    highest = lax.Precision.HIGHEST
    loads_block = rhs[0, 0]
    diag_inverse = inverse[0, 0]
    blocks = factor[0, 0]
    targets = pattern[0, 0]
    loads, width = loads_block.shape
    place = lax.axis_index("chain")
    onehot = (targets[:, None] == jnp.arange(supers, dtype=jnp.int32)[None, :]).astype(jnp.float32)
    pieces = 1
    rows = loads // pieces
    steps = levels + pieces - 1

    def window(step, lag):
        index = step - lag
        live = (index >= 0) & (index < pieces)
        start = jnp.clip(index, 0, pieces - 1) * rows
        return (live, start)

    def forward_step(step, carry):
        solved, incoming = carry
        live, start = window(step, place)
        residue = loads_block - incoming
        fresh = jnp.dot(residue, diag_inverse.T, precision=highest)
        solved = jnp.where(live, fresh, solved)
        terms = jnp.einsum("rb,kab->kra", fresh, blocks, precision=highest)
        summed_rows = lax.psum_scatter(
            jnp.einsum("kc,kra->cra", onehot, terms, precision=highest),
            "col",
            scatter_dimension=0,
            tiled=True,
        )[0]
        arrived = shifted(summed_rows, "chain", 1)
        got, into = window(step + 1, place)
        got = got & (place > 0)
        incoming = jnp.where(got, arrived, incoming)
        return (solved, incoming)

    empty = jnp.zeros((loads, width), jnp.float32)
    solved, unused = lax.fori_loop(0, steps, forward_step, (empty, empty))

    def backward_step(step, carry):
        answer, outgoing = carry
        lag = levels - 1 - place
        live, start = window(step, lag)
        residue = solved - outgoing
        fresh = jnp.dot(residue, diag_inverse, precision=highest)
        answer = jnp.where(live, fresh, answer)
        arrived = shifted(fresh, "chain", -1)
        picked = jnp.einsum(
            "kc,cra->kra",
            onehot,
            lax.all_gather(arrived[None], "col", axis=0, tiled=True),
            precision=highest,
        )
        term = jnp.einsum("kra,kab->rb", picked, blocks, precision=highest)
        got, into = window(step, lag - 1)
        got = got & (place < levels - 1)
        outgoing = jnp.where(got, term, outgoing)
        return (answer, outgoing)

    answer, unused_rows = lax.fori_loop(0, steps, backward_step, (empty, empty))
    return (solved[None, None], answer[None, None])


def solution(mesh):
    in_specs = (
        P("chain", "col", None, None),
        P("chain", "col", None, None),
        P("chain", "col", None, None, None),
        P("chain", "col", None),
    )
    out_specs = (P("chain", "col", None, None), P("chain", "col", None, None))
    return jax.shard_map(body, mesh=mesh, in_specs=in_specs, out_specs=out_specs, check_vma=False)
```

profile of v0, /device:TPU:2, one launch (start us, length us, event | category | flops | bytes accessed | tf_op | source)
XLA Modules:
  0.0 2476.0 jit_solution(1854762112092310647)
XLA Ops:
  7.8 1795.3 %while.35 = (s32[]{:T(128)}, f32[64,128]{1,0:T(8,128)S(1)}, f32[64,128]{1,0:T(8,128)S(1)}, s32[]{:T(128)}, f32[64,128]{1,0:T(8,128)}, /*index=5*/f32[128,128]{1,...) while((s32[]{:T(128)}, f32[64,128]{1,0:T(8,128)S(1)}, ...), condition=%wide.region_2.3_spmd.clone, body=%wide.region_0.2_spmd.clone.sunk | while | flops 138461696 | bytes 7930159 | solution.py:54
  13.4 217.5 %reduce-scatter.2.cloned.1.call-done = f32[1,64,128]{2,1,0:T(8,128)} async-done(((f32[32,64,128]{2,1,0:T(8,128)}), f32[1,64,128]{2,1,0:T(8,128)}) %reduce-scatter.2.cloned.1.call-update) | async-done | bytes 32784 | tf_op jit(solution)/shard_map/while/body/eval_jaxpr/reduce_scatter | solution.py:41
  232.8 3.5 collective-permute-done
  241.9 212.8 %reduce-scatter.2.cloned.1.call-done = f32[1,64,128]{2,1,0:T(8,128)} async-done(((f32[32,64,128]{2,1,0:T(8,128)}), f32[1,64,128]{2,1,0:T(8,128)}) %reduce-scatter.2.cloned.1.call-update) | async-done | bytes 32784 | tf_op jit(solution)/shard_map/while/body/eval_jaxpr/reduce_scatter | solution.py:41
  456.6 3.5 collective-permute-done
  465.7 212.8 %reduce-scatter.2.cloned.1.call-done = f32[1,64,128]{2,1,0:T(8,128)} async-done(((f32[32,64,128]{2,1,0:T(8,128)}), f32[1,64,128]{2,1,0:T(8,128)}) %reduce-scatter.2.cloned.1.call-update) | async-done | bytes 32784 | tf_op jit(solution)/shard_map/while/body/eval_jaxpr/reduce_scatter | solution.py:41
  680.4 3.5 collective-permute-done
  689.5 212.8 %reduce-scatter.2.cloned.1.call-done = f32[1,64,128]{2,1,0:T(8,128)} async-done(((f32[32,64,128]{2,1,0:T(8,128)}), f32[1,64,128]{2,1,0:T(8,128)}) %reduce-scatter.2.cloned.1.call-update) | async-done | bytes 32784 | tf_op jit(solution)/shard_map/while/body/eval_jaxpr/reduce_scatter | solution.py:41
  904.2 3.5 collective-permute-done
  913.3 212.8 %reduce-scatter.2.cloned.1.call-done = f32[1,64,128]{2,1,0:T(8,128)} async-done(((f32[32,64,128]{2,1,0:T(8,128)}), f32[1,64,128]{2,1,0:T(8,128)}) %reduce-scatter.2.cloned.1.call-update) | async-done | bytes 32784 | tf_op jit(solution)/shard_map/while/body/eval_jaxpr/reduce_scatter | solution.py:41
  1128.1 3.5 collective-permute-done
  1137.2 212.9 %reduce-scatter.2.cloned.1.call-done = f32[1,64,128]{2,1,0:T(8,128)} async-done(((f32[32,64,128]{2,1,0:T(8,128)}), f32[1,64,128]{2,1,0:T(8,128)}) %reduce-scatter.2.cloned.1.call-update) | async-done | bytes 32784 | tf_op jit(solution)/shard_map/while/body/eval_jaxpr/reduce_scatter | solution.py:41
  1352.0 3.5 collective-permute-done
  1361.1 212.8 %reduce-scatter.2.cloned.1.call-done = f32[1,64,128]{2,1,0:T(8,128)} async-done(((f32[32,64,128]{2,1,0:T(8,128)}), f32[1,64,128]{2,1,0:T(8,128)}) %reduce-scatter.2.cloned.1.call-update) | async-done | bytes 32784 | tf_op jit(solution)/shard_map/while/body/eval_jaxpr/reduce_scatter | solution.py:41
  1575.8 3.5 collective-permute-done
  1584.9 212.7 %reduce-scatter.2.cloned.1.call-done = f32[1,64,128]{2,1,0:T(8,128)} async-done(((f32[32,64,128]{2,1,0:T(8,128)}), f32[1,64,128]{2,1,0:T(8,128)}) %reduce-scatter.2.cloned.1.call-update) | async-done | bytes 32784 | tf_op jit(solution)/shard_map/while/body/eval_jaxpr/reduce_scatter | solution.py:41
  1799.6 3.5 collective-permute-done
  1803.1 665.7 %while.36 = (s32[]{:T(128)}, f32[64,128]{1,0:T(8,128)S(1)}, f32[64,128]{1,0:T(8,128)S(1)}, s32[]{:T(128)}, f32[64,128]{1,0:T(8,128)S(1)}, /*index=5*/f32[128,128...) while((s32[]{:T(128)}, f32[64,128]{1,0:T(8,128)S(1)}, ...), condition=%wide.region_4.5_spmd.clone, body=%wide.region_3.4_spmd.clone.sunk | while | flops 138461696 | bytes 7995759 | solution.py:76
  1808.4 75.5 %all-gather.6.cloned.1.call-done = f32[2048,128]{1,0:T(8,128)} async-done(((f32[64,128]{1,0:T(8,128)}), f32[2048,128]{1,0:T(8,128)}) %all-gather.6.cloned.1.call-update) | async-done | bytes 1048592 | tf_op jit(solution)/shard_map/while/body/eval_jaxpr/all_gather | solution.py:67
  1883.9 2.5 fusion.59
  1892.2 74.9 %all-gather.6.cloned.1.call-done = f32[2048,128]{1,0:T(8,128)} async-done(((f32[64,128]{1,0:T(8,128)}), f32[2048,128]{1,0:T(8,128)}) %all-gather.6.cloned.1.call-update) | async-done | bytes 1048592 | tf_op jit(solution)/shard_map/while/body/eval_jaxpr/all_gather | solution.py:67
  1967.0 2.5 fusion.59
  1975.3 74.9 %all-gather.6.cloned.1.call-done = f32[2048,128]{1,0:T(8,128)} async-done(((f32[64,128]{1,0:T(8,128)}), f32[2048,128]{1,0:T(8,128)}) %all-gather.6.cloned.1.call-update) | async-done | bytes 1048592 | tf_op jit(solution)/shard_map/while/body/eval_jaxpr/all_gather | solution.py:67
  2050.2 2.5 fusion.59
  2058.4 74.9 %all-gather.6.cloned.1.call-done = f32[2048,128]{1,0:T(8,128)} async-done(((f32[64,128]{1,0:T(8,128)}), f32[2048,128]{1,0:T(8,128)}) %all-gather.6.cloned.1.call-update) | async-done | bytes 1048592 | tf_op jit(solution)/shard_map/while/body/eval_jaxpr/all_gather | solution.py:67
  2133.3 2.5 fusion.59
  2141.5 74.9 %all-gather.6.cloned.1.call-done = f32[2048,128]{1,0:T(8,128)} async-done(((f32[64,128]{1,0:T(8,128)}), f32[2048,128]{1,0:T(8,128)}) %all-gather.6.cloned.1.call-update) | async-done | bytes 1048592 | tf_op jit(solution)/shard_map/while/body/eval_jaxpr/all_gather | solution.py:67
  2224.7 74.9 %all-gather.6.cloned.1.call-done = f32[2048,128]{1,0:T(8,128)} async-done(((f32[64,128]{1,0:T(8,128)}), f32[2048,128]{1,0:T(8,128)}) %all-gather.6.cloned.1.call-update) | async-done | bytes 1048592 | tf_op jit(solution)/shard_map/while/body/eval_jaxpr/all_gather | solution.py:67
  2299.6 2.5 fusion.59
  2307.8 74.9 %all-gather.6.cloned.1.call-done = f32[2048,128]{1,0:T(8,128)} async-done(((f32[64,128]{1,0:T(8,128)}), f32[2048,128]{1,0:T(8,128)}) %all-gather.6.cloned.1.call-update) | async-done | bytes 1048592 | tf_op jit(solution)/shard_map/while/body/eval_jaxpr/all_gather | solution.py:67
  2390.9 74.9 %all-gather.6.cloned.1.call-done = f32[2048,128]{1,0:T(8,128)} async-done(((f32[64,128]{1,0:T(8,128)}), f32[2048,128]{1,0:T(8,128)}) %all-gather.6.cloned.1.call-update) | async-done | bytes 1048592 | tf_op jit(solution)/shard_map/while/body/eval_jaxpr/all_gather | solution.py:67
  2465.8 2.5 fusion.59
  (156 shorter events, 111.3 us)
Async XLA Ops:
  7.8 223.0 %reduce-scatter.2.cloned.1.call-start = ((), (), s32[]{:S(2)}) async-start(), calls=%async_computation.1 | async-start | bytes 1081344 | tf_op jit(solution)/shard_map/while/body/eval_jaxpr/reduce_scatter | solution.py:41
  230.8 5.4 collective-permute-start
  236.3 218.4 %reduce-scatter.2.cloned.1.call-start = ((), (), s32[]{:S(2)}) async-start(), calls=%async_computation.1 | async-start | bytes 1081344 | tf_op jit(solution)/shard_map/while/body/eval_jaxpr/reduce_scatter | solution.py:41
  454.7 5.4 collective-permute-start
  460.1 218.4 %reduce-scatter.2.cloned.1.call-start = ((), (), s32[]{:S(2)}) async-start(), calls=%async_computation.1 | async-start | bytes 1081344 | tf_op jit(solution)/shard_map/while/body/eval_jaxpr/reduce_scatter | solution.py:41
  678.5 5.4 collective-permute-start
  683.9 218.3 %reduce-scatter.2.cloned.1.call-start = ((), (), s32[]{:S(2)}) async-start(), calls=%async_computation.1 | async-start | bytes 1081344 | tf_op jit(solution)/shard_map/while/body/eval_jaxpr/reduce_scatter | solution.py:41
  902.3 5.4 collective-permute-start
  907.7 218.4 %reduce-scatter.2.cloned.1.call-start = ((), (), s32[]{:S(2)}) async-start(), calls=%async_computation.1 | async-start | bytes 1081344 | tf_op jit(solution)/shard_map/while/body/eval_jaxpr/reduce_scatter | solution.py:41
  1126.2 5.4 collective-permute-start
  1131.6 218.5 %reduce-scatter.2.cloned.1.call-start = ((), (), s32[]{:S(2)}) async-start(), calls=%async_computation.1 | async-start | bytes 1081344 | tf_op jit(solution)/shard_map/while/body/eval_jaxpr/reduce_scatter | solution.py:41
  1350.1 5.4 collective-permute-start
  1355.5 218.4 %reduce-scatter.2.cloned.1.call-start = ((), (), s32[]{:S(2)}) async-start(), calls=%async_computation.1 | async-start | bytes 1081344 | tf_op jit(solution)/shard_map/while/body/eval_jaxpr/reduce_scatter | solution.py:41
  1573.9 5.4 collective-permute-start
  1579.3 218.3 %reduce-scatter.2.cloned.1.call-start = ((), (), s32[]{:S(2)}) async-start(), calls=%async_computation.1 | async-start | bytes 1081344 | tf_op jit(solution)/shard_map/while/body/eval_jaxpr/reduce_scatter | solution.py:41
  1797.7 5.4 collective-permute-start
  1803.1 80.8 %all-gather.6.cloned.1.call-start = ((), (), s32[]{:S(2)}) async-start(), calls=%async_computation.2 | async-start | bytes 1081344 | tf_op jit(solution)/shard_map/while/body/eval_jaxpr/all_gather | solution.py:67
  1804.2 3.5 collective-permute-start.1
  1886.9 80.1 %all-gather.6.cloned.1.call-start = ((), (), s32[]{:S(2)}) async-start(), calls=%async_computation.2 | async-start | bytes 1081344 | tf_op jit(solution)/shard_map/while/body/eval_jaxpr/all_gather | solution.py:67
  1888.0 3.5 collective-permute-start.1
  1970.0 80.1 %all-gather.6.cloned.1.call-start = ((), (), s32[]{:S(2)}) async-start(), calls=%async_computation.2 | async-start | bytes 1081344 | tf_op jit(solution)/shard_map/while/body/eval_jaxpr/all_gather | solution.py:67
  1971.1 3.5 collective-permute-start.1
  2053.2 80.1 %all-gather.6.cloned.1.call-start = ((), (), s32[]{:S(2)}) async-start(), calls=%async_computation.2 | async-start | bytes 1081344 | tf_op jit(solution)/shard_map/while/body/eval_jaxpr/all_gather | solution.py:67
  2054.3 3.5 collective-permute-start.1
  2136.3 80.1 %all-gather.6.cloned.1.call-start = ((), (), s32[]{:S(2)}) async-start(), calls=%async_computation.2 | async-start | bytes 1081344 | tf_op jit(solution)/shard_map/while/body/eval_jaxpr/all_gather | solution.py:67
  2137.4 3.5 collective-permute-start.1
  2219.4 80.1 %all-gather.6.cloned.1.call-start = ((), (), s32[]{:S(2)}) async-start(), calls=%async_computation.2 | async-start | bytes 1081344 | tf_op jit(solution)/shard_map/while/body/eval_jaxpr/all_gather | solution.py:67
  2220.5 3.5 collective-permute-start.1
  2302.6 80.1 %all-gather.6.cloned.1.call-start = ((), (), s32[]{:S(2)}) async-start(), calls=%async_computation.2 | async-start | bytes 1081344 | tf_op jit(solution)/shard_map/while/body/eval_jaxpr/all_gather | solution.py:67
  2303.7 3.5 collective-permute-start.1
  2385.7 80.1 %all-gather.6.cloned.1.call-start = ((), (), s32[]{:S(2)}) async-start(), calls=%async_computation.2 | async-start | bytes 1081344 | tf_op jit(solution)/shard_map/while/body/eval_jaxpr/all_gather | solution.py:67
  2386.8 3.5 collective-permute-start.1
  (19 other events, 26.8 us)
Sparse Core Ops, SparseCore 0:
  13.5 217.2 reduce-scatter.1
  242.0 212.6 reduce-scatter.1
  465.8 212.6 reduce-scatter.1
  689.7 212.5 reduce-scatter.1
  913.4 212.6 reduce-scatter.1
  1137.3 212.6 reduce-scatter.1
  1361.2 212.6 reduce-scatter.1
  1585.1 212.5 reduce-scatter.1
  1808.5 75.3 all-gather.5
  1892.3 74.7 all-gather.5
  1975.4 74.7 all-gather.5
  2058.5 74.7 all-gather.5
  2141.7 74.7 all-gather.5
  2224.8 74.7 all-gather.5
  2307.9 74.7 all-gather.5
  2391.0 74.7 all-gather.5
where the time goes:
time: 2480 us
  waiting for transfers between devices  2350 us (95%)
  matrix products  63.1 us (3%)
  starting transfers between devices  31.2 us (1%)
    reduce_scatter x8, waiting for transfers between devices, forward_step(): lax.psum_scatter(jnp.einsum('kc,kra->cra', onehot, terms, precision=highe...  1710 us
    all_gather x8, waiting for transfers between devices, backward_step(): lax.all_gather(arrived[None], 'col', axis=0, tiled=True)  600 us
  transfers between devices with their start and end apart: 32, of which 32 were waited for; matrix products, arithmetic and copies ran while one was open for 0% of the time, Pallas kernels for 0%

commit v1 on v0

--- a/solution.py
+++ b/solution.py
@@ -64,7 +64,10 @@
         picked = jnp.einsum(
             "kc,cra->kra",
             onehot,
-            lax.all_gather(arrived[None], "col", axis=0, tiled=True),
+            jnp.concatenate(
+                lax.all_to_all(jnp.stack([arrived[None]] * lax.axis_size("col")), "col", 0, 0),
+                axis=0,
+            ),
             precision=highest,
         )
         term = jnp.einsum("kra,kab->rb", picked, blocks, precision=highest)

time: 2480 us -> 2150 us (0.87)
  waiting for transfers between devices: 2350 us -> 1970 us
  starting transfers between devices: 31.2 us -> 80.9 us
    all_gather x8 -> x0, waiting for transfers between devices: 600 us -> none  [backward_step(): lax.all_gather(arrived[None], 'col', axis=0, tiled=True)]
    all_to_all x0 -> x8, waiting for transfers between devices: none -> 215 us  [backward_step(): lax.all_to_all(jnp.stack([arrived[None]] * lax.axis_size('col')), 'col',...]
    all_to_all x0 -> x8, starting transfers between devices: none -> 49 us  [backward_step(): lax.all_to_all(jnp.stack([arrived[None]] * lax.axis_size('col')), 'col',...]
where the time goes in v1:
time: 2150 us
  waiting for transfers between devices  1970 us (92%)
  starting transfers between devices  80.9 us (4%)
  matrix products  53.1 us (2%)
  local copies, waits for them, and re-layouts  22.7 us (1%)
    reduce_scatter x8, waiting for transfers between devices, forward_step(): lax.psum_scatter(jnp.einsum('kc,kra->cra', onehot, terms, precision=highe...  1710 us
    all_to_all x8, waiting for transfers between devices, backward_step(): lax.all_to_all(jnp.stack([arrived[None]] * lax.axis_size('col')), 'col',...  215 us
    ppermute x16, waiting for transfers between devices, shifted(): lax.ppermute(value, axis, [(source, source + steps) for source in range(f...  52.2 us
    all_to_all x8, starting transfers between devices, backward_step(): lax.all_to_all(jnp.stack([arrived[None]] * lax.axis_size('col')), 'col',...  49 us
  transfers between devices with their start and end apart: 32, of which 32 were waited for; matrix products, arithmetic and copies ran while one was open for 0% of the time, Pallas kernels for 0%

profile of v1, /device:TPU:2, one launch (start us, length us, event | category | flops | bytes accessed | tf_op | source)
XLA Modules:
  0.0 2146.9 jit_solution(5772110562407181234)
XLA Ops:
  7.8 1795.2 %while.35 = (s32[]{:T(128)}, f32[64,128]{1,0:T(8,128)S(1)}, f32[64,128]{1,0:T(8,128)S(1)}, s32[]{:T(128)}, f32[64,128]{1,0:T(8,128)}, /*index=5*/f32[128,128]{1,...) while((s32[]{:T(128)}, f32[64,128]{1,0:T(8,128)S(1)}, ...), condition=%wide.region_2.3_spmd.clone, body=%wide.region_0.2_spmd.clone.sunk | while | flops 138461696 | bytes 7930159 | solution.py:54
  13.4 217.5 %reduce-scatter.2.cloned.1.call-done = f32[1,64,128]{2,1,0:T(8,128)} async-done(((f32[32,64,128]{2,1,0:T(8,128)}), f32[1,64,128]{2,1,0:T(8,128)}) %reduce-scatter.2.cloned.1.call-update) | async-done | bytes 32784 | tf_op jit(solution)/shard_map/while/body/eval_jaxpr/reduce_scatter | solution.py:41
  232.8 3.5 collective-permute-done
  241.9 212.8 %reduce-scatter.2.cloned.1.call-done = f32[1,64,128]{2,1,0:T(8,128)} async-done(((f32[32,64,128]{2,1,0:T(8,128)}), f32[1,64,128]{2,1,0:T(8,128)}) %reduce-scatter.2.cloned.1.call-update) | async-done | bytes 32784 | tf_op jit(solution)/shard_map/while/body/eval_jaxpr/reduce_scatter | solution.py:41
  456.6 3.5 collective-permute-done
  465.7 212.8 %reduce-scatter.2.cloned.1.call-done = f32[1,64,128]{2,1,0:T(8,128)} async-done(((f32[32,64,128]{2,1,0:T(8,128)}), f32[1,64,128]{2,1,0:T(8,128)}) %reduce-scatter.2.cloned.1.call-update) | async-done | bytes 32784 | tf_op jit(solution)/shard_map/while/body/eval_jaxpr/reduce_scatter | solution.py:41
  689.5 212.8 %reduce-scatter.2.cloned.1.call-done = f32[1,64,128]{2,1,0:T(8,128)} async-done(((f32[32,64,128]{2,1,0:T(8,128)}), f32[1,64,128]{2,1,0:T(8,128)}) %reduce-scatter.2.cloned.1.call-update) | async-done | bytes 32784 | tf_op jit(solution)/shard_map/while/body/eval_jaxpr/reduce_scatter | solution.py:41
  913.3 212.7 %reduce-scatter.2.cloned.1.call-done = f32[1,64,128]{2,1,0:T(8,128)} async-done(((f32[32,64,128]{2,1,0:T(8,128)}), f32[1,64,128]{2,1,0:T(8,128)}) %reduce-scatter.2.cloned.1.call-update) | async-done | bytes 32784 | tf_op jit(solution)/shard_map/while/body/eval_jaxpr/reduce_scatter | solution.py:41
  1137.1 212.8 %reduce-scatter.2.cloned.1.call-done = f32[1,64,128]{2,1,0:T(8,128)} async-done(((f32[32,64,128]{2,1,0:T(8,128)}), f32[1,64,128]{2,1,0:T(8,128)}) %reduce-scatter.2.cloned.1.call-update) | async-done | bytes 32784 | tf_op jit(solution)/shard_map/while/body/eval_jaxpr/reduce_scatter | solution.py:41
  1361.0 212.8 %reduce-scatter.2.cloned.1.call-done = f32[1,64,128]{2,1,0:T(8,128)} async-done(((f32[32,64,128]{2,1,0:T(8,128)}), f32[1,64,128]{2,1,0:T(8,128)}) %reduce-scatter.2.cloned.1.call-update) | async-done | bytes 32784 | tf_op jit(solution)/shard_map/while/body/eval_jaxpr/reduce_scatter | solution.py:41
  1584.8 212.7 %reduce-scatter.2.cloned.1.call-done = f32[1,64,128]{2,1,0:T(8,128)} async-done(((f32[32,64,128]{2,1,0:T(8,128)}), f32[1,64,128]{2,1,0:T(8,128)}) %reduce-scatter.2.cloned.1.call-update) | async-done | bytes 32784 | tf_op jit(solution)/shard_map/while/body/eval_jaxpr/reduce_scatter | solution.py:41
  1803.0 336.4 %while.36 = (s32[]{:T(128)}, f32[64,128]{1,0:T(8,128)S(1)}, f32[64,128]{1,0:T(8,128)S(1)}, s32[]{:T(128)}, f32[64,128]{1,0:T(8,128)S(1)}, /*index=5*/f32[128,128...) while((s32[]{:T(128)}, f32[64,128]{1,0:T(8,128)S(1)}, ...), condition=%wide.region_4.5_spmd.clone, body=%wide.region_3.4_spmd.clone.sunk | while | flops 138461696 | bytes 8847691 | solution.py:79
  1808.7 6.8 all-to-all-start
  1815.5 28.2 %all-to-all-done = f32[32,1,64,128]{3,2,1,0:T(8,128)S(1)} async-done(((f32[32,1,64,128]{3,2,1,0:T(8,128)}), f32[32,1,64,128]{3,2,1,0:T(8,128)S(1)}, u32[]{:S(2)}, u32[]{:S(2)}) %all-to-all-start) | async-done | bytes 1048608 | tf_op jit(solution)/shard_map/while/body/eval_jaxpr/all_to_all | solution.py:68
  1851.6 6.3 all-to-all-start
  1857.9 27.0 %all-to-all-done = f32[32,1,64,128]{3,2,1,0:T(8,128)S(1)} async-done(((f32[32,1,64,128]{3,2,1,0:T(8,128)}), f32[32,1,64,128]{3,2,1,0:T(8,128)S(1)}, u32[]{:S(2)}, u32[]{:S(2)}) %all-to-all-start) | async-done | bytes 1048608 | tf_op jit(solution)/shard_map/while/body/eval_jaxpr/all_to_all | solution.py:68
  1894.1 6.1 all-to-all-start
  1900.2 26.9 %all-to-all-done = f32[32,1,64,128]{3,2,1,0:T(8,128)S(1)} async-done(((f32[32,1,64,128]{3,2,1,0:T(8,128)}), f32[32,1,64,128]{3,2,1,0:T(8,128)S(1)}, u32[]{:S(2)}, u32[]{:S(2)}) %all-to-all-start) | async-done | bytes 1048608 | tf_op jit(solution)/shard_map/while/body/eval_jaxpr/all_to_all | solution.py:68
  1936.4 6.0 all-to-all-start
  1942.5 26.8 %all-to-all-done = f32[32,1,64,128]{3,2,1,0:T(8,128)S(1)} async-done(((f32[32,1,64,128]{3,2,1,0:T(8,128)}), f32[32,1,64,128]{3,2,1,0:T(8,128)S(1)}, u32[]{:S(2)}, u32[]{:S(2)}) %all-to-all-start) | async-done | bytes 1048608 | tf_op jit(solution)/shard_map/while/body/eval_jaxpr/all_to_all | solution.py:68
  1974.0 3.5 collective-permute-done.1
  1978.7 6.0 all-to-all-start
  1984.7 26.8 %all-to-all-done = f32[32,1,64,128]{3,2,1,0:T(8,128)S(1)} async-done(((f32[32,1,64,128]{3,2,1,0:T(8,128)}), f32[32,1,64,128]{3,2,1,0:T(8,128)S(1)}, u32[]{:S(2)}, u32[]{:S(2)}) %all-to-all-start) | async-done | bytes 1048608 | tf_op jit(solution)/shard_map/while/body/eval_jaxpr/all_to_all | solution.py:68
  2016.2 3.6 collective-permute-done.1
  2020.9 6.0 all-to-all-start
  2026.9 26.7 %all-to-all-done = f32[32,1,64,128]{3,2,1,0:T(8,128)S(1)} async-done(((f32[32,1,64,128]{3,2,1,0:T(8,128)}), f32[32,1,64,128]{3,2,1,0:T(8,128)S(1)}, u32[]{:S(2)}, u32[]{:S(2)}) %all-to-all-start) | async-done | bytes 1048608 | tf_op jit(solution)/shard_map/while/body/eval_jaxpr/all_to_all | solution.py:68
  2058.4 3.7 collective-permute-done.1
  2063.2 5.9 all-to-all-start
  2069.2 26.6 %all-to-all-done = f32[32,1,64,128]{3,2,1,0:T(8,128)S(1)} async-done(((f32[32,1,64,128]{3,2,1,0:T(8,128)}), f32[32,1,64,128]{3,2,1,0:T(8,128)S(1)}, u32[]{:S(2)}, u32[]{:S(2)}) %all-to-all-start) | async-done | bytes 1048608 | tf_op jit(solution)/shard_map/while/body/eval_jaxpr/all_to_all | solution.py:68
  2100.5 3.8 collective-permute-done.1
  2105.4 5.9 all-to-all-start
  2111.3 26.4 %all-to-all-done = f32[32,1,64,128]{3,2,1,0:T(8,128)S(1)} async-done(((f32[32,1,64,128]{3,2,1,0:T(8,128)}), f32[32,1,64,128]{3,2,1,0:T(8,128)S(1)}, u32[]{:S(2)}, u32[]{:S(2)}) %all-to-all-start) | async-done | bytes 1048608 | tf_op jit(solution)/shard_map/while/body/eval_jaxpr/all_to_all | solution.py:68
  (140 shorter events, 138.4 us)
Async XLA Ops:
  7.8 223.0 %reduce-scatter.2.cloned.1.call-start = ((), (), s32[]{:S(2)}) async-start(), calls=%async_computation.2 | async-start | bytes 1081344 | tf_op jit(solution)/shard_map/while/body/eval_jaxpr/reduce_scatter | solution.py:41
  230.9 5.4 collective-permute-start
  236.3 218.3 %reduce-scatter.2.cloned.1.call-start = ((), (), s32[]{:S(2)}) async-start(), calls=%async_computation.2 | async-start | bytes 1081344 | tf_op jit(solution)/shard_map/while/body/eval_jaxpr/reduce_scatter | solution.py:41
  454.6 5.4 collective-permute-start
  460.1 218.4 %reduce-scatter.2.cloned.1.call-start = ((), (), s32[]{:S(2)}) async-start(), calls=%async_computation.2 | async-start | bytes 1081344 | tf_op jit(solution)/shard_map/while/body/eval_jaxpr/reduce_scatter | solution.py:41
  678.5 5.4 collective-permute-start
  683.9 218.4 %reduce-scatter.2.cloned.1.call-start = ((), (), s32[]{:S(2)}) async-start(), calls=%async_computation.2 | async-start | bytes 1081344 | tf_op jit(solution)/shard_map/while/body/eval_jaxpr/reduce_scatter | solution.py:41
  902.3 5.4 collective-permute-start
  907.7 218.3 %reduce-scatter.2.cloned.1.call-start = ((), (), s32[]{:S(2)}) async-start(), calls=%async_computation.2 | async-start | bytes 1081344 | tf_op jit(solution)/shard_map/while/body/eval_jaxpr/reduce_scatter | solution.py:41
  1126.1 5.4 collective-permute-start
  1131.5 218.4 %reduce-scatter.2.cloned.1.call-start = ((), (), s32[]{:S(2)}) async-start(), calls=%async_computation.2 | async-start | bytes 1081344 | tf_op jit(solution)/shard_map/while/body/eval_jaxpr/reduce_scatter | solution.py:41
  1349.9 5.4 collective-permute-start
  1355.4 218.4 %reduce-scatter.2.cloned.1.call-start = ((), (), s32[]{:S(2)}) async-start(), calls=%async_computation.2 | async-start | bytes 1081344 | tf_op jit(solution)/shard_map/while/body/eval_jaxpr/reduce_scatter | solution.py:41
  1573.8 5.4 collective-permute-start
  1579.2 218.3 %reduce-scatter.2.cloned.1.call-start = ((), (), s32[]{:S(2)}) async-start(), calls=%async_computation.2 | async-start | bytes 1081344 | tf_op jit(solution)/shard_map/while/body/eval_jaxpr/reduce_scatter | solution.py:41
  1797.6 5.4 collective-permute-start
  1804.1 3.5 collective-permute-start.1
  1808.7 35.1 %all-to-all-start = ((f32[32,1,64,128]{3,2,1,0:T(8,128)}), f32[32,1,64,128]{3,2,1,0:T(8,128)S(1)}, u32[]{:S(2)}, u32[]{:S(2)}) async-start(f32[32,1,64,128]{3,2,1,0:T(8,128)} %stack.7), calls=%async_computation.1 | async-start | bytes 2097152 | tf_op jit(solution)/shard_map/while/body/eval_jaxpr/all_to_all | solution.py:68
  1846.6 4.0 collective-permute-start.1
  1851.6 33.3 %all-to-all-start = ((f32[32,1,64,128]{3,2,1,0:T(8,128)}), f32[32,1,64,128]{3,2,1,0:T(8,128)S(1)}, u32[]{:S(2)}, u32[]{:S(2)}) async-start(f32[32,1,64,128]{3,2,1,0:T(8,128)} %stack.7), calls=%async_computation.1 | async-start | bytes 2097152 | tf_op jit(solution)/shard_map/while/body/eval_jaxpr/all_to_all | solution.py:68
  1887.7 5.3 collective-permute-start.1
  1894.1 33.0 %all-to-all-start = ((f32[32,1,64,128]{3,2,1,0:T(8,128)}), f32[32,1,64,128]{3,2,1,0:T(8,128)S(1)}, u32[]{:S(2)}, u32[]{:S(2)}) async-start(f32[32,1,64,128]{3,2,1,0:T(8,128)} %stack.7), calls=%async_computation.1 | async-start | bytes 2097152 | tf_op jit(solution)/shard_map/while/body/eval_jaxpr/all_to_all | solution.py:68
  1929.9 5.4 collective-permute-start.1
  1936.4 32.9 %all-to-all-start = ((f32[32,1,64,128]{3,2,1,0:T(8,128)}), f32[32,1,64,128]{3,2,1,0:T(8,128)S(1)}, u32[]{:S(2)}, u32[]{:S(2)}) async-start(f32[32,1,64,128]{3,2,1,0:T(8,128)} %stack.7), calls=%async_computation.1 | async-start | bytes 2097152 | tf_op jit(solution)/shard_map/while/body/eval_jaxpr/all_to_all | solution.py:68
  1972.1 5.5 collective-permute-start.1
  1978.7 32.8 %all-to-all-start = ((f32[32,1,64,128]{3,2,1,0:T(8,128)}), f32[32,1,64,128]{3,2,1,0:T(8,128)S(1)}, u32[]{:S(2)}, u32[]{:S(2)}) async-start(f32[32,1,64,128]{3,2,1,0:T(8,128)} %stack.7), calls=%async_computation.1 | async-start | bytes 2097152 | tf_op jit(solution)/shard_map/while/body/eval_jaxpr/all_to_all | solution.py:68
  2014.3 5.5 collective-permute-start.1
  2020.9 32.7 %all-to-all-start = ((f32[32,1,64,128]{3,2,1,0:T(8,128)}), f32[32,1,64,128]{3,2,1,0:T(8,128)S(1)}, u32[]{:S(2)}, u32[]{:S(2)}) async-start(f32[32,1,64,128]{3,2,1,0:T(8,128)} %stack.7), calls=%async_computation.1 | async-start | bytes 2097152 | tf_op jit(solution)/shard_map/while/body/eval_jaxpr/all_to_all | solution.py:68
  2056.5 5.6 collective-permute-start.1
  2063.2 32.6 %all-to-all-start = ((f32[32,1,64,128]{3,2,1,0:T(8,128)}), f32[32,1,64,128]{3,2,1,0:T(8,128)S(1)}, u32[]{:S(2)}, u32[]{:S(2)}) async-start(f32[32,1,64,128]{3,2,1,0:T(8,128)} %stack.7), calls=%async_computation.1 | async-start | bytes 2097152 | tf_op jit(solution)/shard_map/while/body/eval_jaxpr/all_to_all | solution.py:68
  2098.6 5.8 collective-permute-start.1
  2105.4 32.3 %all-to-all-start = ((f32[32,1,64,128]{3,2,1,0:T(8,128)}), f32[32,1,64,128]{3,2,1,0:T(8,128)S(1)}, u32[]{:S(2)}, u32[]{:S(2)}) async-start(f32[32,1,64,128]{3,2,1,0:T(8,128)} %stack.7), calls=%async_computation.1 | async-start | bytes 2097152 | tf_op jit(solution)/shard_map/while/body/eval_jaxpr/all_to_all | solution.py:68
  (11 other events, 11.9 us)
Sparse Core Ops, SparseCore 0:
  13.5 217.3 reduce-scatter.1
  242.0 212.5 reduce-scatter.1
  465.8 212.6 reduce-scatter.1
  689.6 212.6 reduce-scatter.1
  913.5 212.5 reduce-scatter.1
  1137.2 212.6 reduce-scatter.1
  1361.1 212.6 reduce-scatter.1
  1584.9 212.5 reduce-scatter.1
